TPU v7x, 32 devices: a whole 2x2x4 slice. The times are simulated.
32 devices in a mesh: groups: 2 (over x), expert: 16 (over z, y, core).
Axes of the slice: x: 2, y: 2, z: 4, core: 2. Of those that a mesh axis runs over, the one named last changes fastest.
Arguments:
- residual: bfloat16 [4096, 3584], P(('groups', 'expert')), parts along dimension 0, may hold values from -24 to 24
- norm_gain: float32 [3584], replicated, may hold values from 0.25 to 1.75
- router: bfloat16 [3584, 4], replicated, may hold values from -0.09375 to 0.09375
- w_gate: bfloat16 [3584, 4096], P(None, 'expert'), may hold values from -0.09375 to 0.09375
- w_up: bfloat16 [3584, 4096], P(None, 'expert'), may hold values from -0.09375 to 0.09375
- w_down: bfloat16 [4096, 3584], P('expert'), may hold values from -0.1875 to 0.1875
- expert_ids: int32 [4096, 2], P(('groups', 'expert')), parts along dimension 0, may hold values from 0 to 3, all different within a row; in each aligned block of 128 rows (0 to 127, 128 to 255, ...) at most 96 rows name the same one
Outputs:
- layer_out: bfloat16 [4096, 3584], P(('groups', 'expert')), parts along dimension 0
There are 2 independent parts, one for each index of `groups`. A program takes and returns all parts, laid end to end along the dimension named above; an argument that names none is the same for every part. Nothing has to cross between parts.
Inputs may be any that keep to these rules, and one draw needn't show every extreme that they name: `expert_ids`: each row names 2 different experts. Within the rows of one device no expert is named by more than 96 rows, and in every draw some device's rows name some expert exactly 96 times.
All inputs are finite; a program needn't handle non-finite values.
Results may differ from a plain program's by a relative error of at most 0.0054.
Values may be sent and summed in bfloat16 or wider, within the bound.
A program may use at most 128 MiB of HBM per device.

v0:
```python
import jax
import jax.numpy as jnp
from jax import lax
from jax.sharding import PartitionSpec as P

route_scale = 2.5
norm_eps = 1e-06


def swapped(value, axis, distance):
    mask = 2**distance
    pairs = [(source, source ^ mask) for source in range(lax.axis_size(axis))]
    return lax.ppermute(value, axis, pairs)


def shards(residual, norm_gain, router, w_gate, w_up, w_down, expert_ids):
    tok_rows, model_width = residual.shape
    top_count = expert_ids.shape[1]
    expert_count = router.shape[1]
    device_count = lax.axis_size("expert")
    span_size = device_count // expert_count
    capacity = 3 * tok_rows * top_count // (2 * expert_count)
    quarter = capacity // span_size
    residual_wide = residual.astype(jnp.float32)
    mean_square = jnp.mean(residual_wide * residual_wide, axis=1, keepdims=True)
    normed = (residual_wide * lax.rsqrt(mean_square + norm_eps) * norm_gain).astype(jnp.bfloat16)
    logits = jnp.dot(normed, router, preferred_element_type=jnp.float32)
    affinity = jax.nn.sigmoid(logits)
    picked = expert_ids[:, :, None] == lax.iota(jnp.int32, expert_count)[None, None, :]
    chosen = jnp.sum(jnp.where(picked, affinity[:, None, :], 0.0), axis=2)
    gate_values = route_scale * chosen / jnp.sum(chosen, axis=1, keepdims=True)
    flat_pick = picked.reshape(tok_rows * top_count, expert_count).astype(jnp.int32)
    before = jnp.cumsum(flat_pick, axis=0) - flat_pick
    target = expert_ids.reshape(tok_rows * top_count) * capacity + jnp.sum(
        before * flat_pick, axis=1
    )
    places = lax.iota(jnp.int32, expert_count * capacity)
    matches = (target[None, :] == places[:, None]).reshape(
        expert_count * capacity, tok_rows, top_count
    )
    assignment = jnp.sum(matches.astype(jnp.float32), axis=2).astype(jnp.bfloat16)
    packed = jnp.dot(assignment, normed, preferred_element_type=jnp.float32).astype(jnp.bfloat16)
    member = lax.axis_index("expert") % span_size
    outgoing = packed.reshape(device_count, quarter, model_width)
    arrived = lax.all_to_all(outgoing, "expert", split_axis=0, concat_axis=0, tiled=True)
    current = arrived.reshape(device_count, 1, quarter, model_width)
    for level_index in range(span_size.bit_length() - 1):
        incoming = swapped(current, "expert", level_index)
        lower_first = (member >> level_index) % 2 == 0
        first_part = jnp.where(lower_first, current, incoming)
        second_part = jnp.where(lower_first, incoming, current)
        current = jnp.concatenate((first_part, second_part), axis=1)
    arrived = current.reshape(device_count, capacity, model_width)
    sources, slot_rows, unused_width = arrived.shape
    flat_rows = arrived.reshape(sources * slot_rows, model_width)
    gate_proj = jnp.dot(flat_rows, w_gate, preferred_element_type=jnp.float32)
    up_proj = jnp.dot(flat_rows, w_up, preferred_element_type=jnp.float32)
    activated = (jax.nn.silu(gate_proj) * up_proj).astype(jnp.bfloat16)
    partial_value = jnp.dot(activated, w_down, preferred_element_type=jnp.float32).astype(
        jnp.bfloat16
    )
    partials = partial_value.reshape(sources, slot_rows, model_width)
    returned = lax.all_to_all(partials, "expert", split_axis=0, concat_axis=0, tiled=True)
    summed = jnp.sum(
        returned.reshape(expert_count, span_size, capacity, model_width), axis=1, dtype=jnp.float32
    )
    flat_sums = summed.reshape(expert_count * capacity, model_width)
    gathered = jnp.take(flat_sums, target, axis=0).reshape(tok_rows, top_count, model_width)
    branch = jnp.sum(gathered * gate_values[:, :, None], axis=1)
    return (residual_wide + branch).astype(jnp.bfloat16)


def solution(mesh):
    in_specs = (
        P(("groups", "expert"), None),
        P(),
        P(),
        P(None, "expert"),
        P(None, "expert"),
        P("expert", None),
        P(("groups", "expert"), None),
    )
    out_specs = P(("groups", "expert"), None)
    return jax.shard_map(shards, mesh=mesh, in_specs=in_specs, out_specs=out_specs, check_vma=False)
```

profile of v0, /device:TPU:17, one launch (start us, length us, event | category | flops | bytes accessed | tf_op | source)
XLA Modules:
  0.0 517.3 jit_solution(12100820611355460152)
XLA Ops:
  0.0 0.0 copy-start
  0.0 0.9 copy.28
  0.9 0.1 eq.57
  1.1 0.1 reshape.124
  1.2 1.2 reduce-window.6
  2.4 0.1 slice.10
  2.5 0.1 copy.30
  2.7 0.1 copy.31
  2.8 0.1 add_bitcast_fusion
  2.9 0.1 reduce_sum.68
  3.0 0.1 copy.32
  3.1 0.7 compare_and_fusion
  3.8 1.4 fusion
  5.3 2.2 convolution_convert_fusion.1
  7.4 67.3 %all_to_all.10 = bf16[16,24,3584]{2,1,0:T(8,128)(2,1)} all-to-all(bf16[16,24,3584]{2,1,0:T(8,128)(2,1)S(1)} %bitcast.42), channel_id=1, replica_groups=mesh['groups'=2,'expert'=16] {'expert'}, dimensions={0} | all-to-all | bytes 5505024 | tf_op jit(solution)/shard_map/all_to_all | solution.py:45
  74.8 1.0 collective-permute-start
  75.8 5.1 collective-permute-done
  80.9 3.0 broadcast_select_fusion.3
  83.8 0.0 copy-start.2
  83.9 0.0 copy-start.3
  83.9 3.3 pad_maximum_fusion.1
  87.1 0.0 copy-done.2
  87.1 0.8 copy-done.3
  87.9 0.0 collective-permute-start.1
  88.0 120.1 %collective-permute-done.1 = bf16[16,2,24,3584]{3,2,1,0:T(8,128)(2,1)} collective-permute-done((bf16[16,2,24,3584]{3,2,1,0:T(8,128)(2,1)}, bf16[16,2,24,3584]{3,2,1,0:T(8,128)(2,1)}, u32[]{:S(2)}, u32[]{:S(2)}) %collective-permute-start.1) | collective-permute-done | bytes 5505056 | tf_op jit(solution)/shard_map/ppermute | solution.py:13
  208.1 4.7 broadcast_select_fusion.1
  212.8 0.0 copy-start.8
  212.8 1.1 pad_maximum_fusion
  213.9 0.0 copy-start.4
  213.9 4.0 copy-done.4
  217.9 0.0 copy-done.8
  217.9 4.2 fusion.19
  222.2 0.0 copy-done
  222.2 17.4 %convolution_convert_fusion = bf16[1536,3584]{1,0:T(8,128)(2,1)} fusion(bf16[256,3584]{1,0:T(8,128)(2,1)S(1)} %copy-done, f32[1536,256]{1,0:T(8,128)} %fusion.19, bf16[1536,3584]{1,0:T(8,128)(2,1)} %bitcast.41, bf16[3584,256]{1,0:T(8,128)(2,1)} %param.11), kind=kOutput, calls=%fused_computation.2 | convolution fusion | flops 5645008896 | bytes 27262976 | tf_op jit(solution)/shard_map/dot_general | solution.py:59
  239.5 0.0 copy-start.7
  239.5 0.0 copy-start.5
  239.5 0.0 copy-start.6
  239.6 0.0 copy-start.9
  239.6 7.4 %all-to-all-start.1 = ((bf16[16,96,3584]{2,1,0:T(8,128)(2,1)}), bf16[16,96,3584]{2,1,0:T(8,128)(2,1)}, u32[]{:S(2)}, u32[]{:S(2)}) async-start(bf16[16,96,3584]{2,1,0:T(8,128)(2,1)} %bitcast.39), calls=%async_computation.1 | async-start | bytes 22020096 | tf_op jit(solution)/shard_map/all_to_all | solution.py:63
  247.0 0.0 copy-done.7
  247.0 0.1 copy.34
  247.1 0.1 mul.80
  247.3 0.1 copy.33
  247.4 0.0 copy-done.5
  247.4 0.0 copy-done.6
  247.4 0.0 copy-done.9
  247.4 0.4 fusion.6
  247.9 0.1 copy.35
  248.0 237.1 %all-to-all-done.1 = bf16[16,96,3584]{2,1,0:T(8,128)(2,1)} async-done(((bf16[16,96,3584]{2,1,0:T(8,128)(2,1)}), bf16[16,96,3584]{2,1,0:T(8,128)(2,1)}, u32[]{:S(2)}, u32[]{:S(2)}) %all-to-all-start.1) | async-done | bytes 11010080 | tf_op jit(solution)/shard_map/all_to_all | solution.py:63
  485.1 8.8 %convert_reduce_fusion = f32[4,96,3584]{2,1,0:T(8,128)} fusion(bf16[16,96,3584]{2,1,0:T(8,128)(2,1)} %all-to-all-done.1), kind=kLoop, calls=%fused_computation.1 | loop fusion | flops 9633792 | bytes 16515072 | tf_op jit(solution)/shard_map/reduce_sum | solution.py:64
  493.9 7.8 %gather_fusion = f32[256,3584]{1,0:T(8,128)} fusion(f32[384,3584]{1,0:T(8,128)} %bitcast.38, s32[1024]{0:T(1024)S(1)} %pad_clamp_fusion), kind=kCustom, calls=%fused_computation | custom fusion | bytes 7341056 | tf_op jit(solution)/shard_map/jit(_take)/gather | solution.py:68
  501.7 5.5 %gather.7 = f32[128,2,3584]{2,1,0:T(2,128)} reshape(f32[256,3584]{1,0:T(8,128)} %gather_fusion) | data formatting | bytes 7340032 | tf_op jit(solution)/shard_map/jit(_take)/gather | solution.py:68
  507.2 0.0 copy-start.1
  507.2 9.0 %multiply_reduce_fusion = f32[128,3584]{1,0:T(8,128)S(1)} fusion(f32[128,2,3584]{2,1,0:T(2,128)} %gather.7, pred[128,2]{1,0:T(8,128)(4,1)S(1)} %copy.33, f32[128,2]{1,0:T(8,128)S(1)} %copy.35), kind=kLoop, calls=%fused_computation.8 | loop fusion | flops 2293760 | bytes 5506304 | tf_op jit(solution)/shard_map/reduce_sum | solution.py:69
  516.2 1.1 fusion.3
  517.3 0.0 copy-done.1
  (11 shorter events, 0.2 us)
Async XLA Ops:
  0.0 222.2 %copy-start = (bf16[256,3584]{1,0:T(8,128)(2,1)S(1)}, bf16[256,3584]{1,0:T(8,128)(2,1)}, u32[]{:S(2)}) copy-start(bf16[256,3584]{1,0:T(8,128)(2,1)} %param.12) | copy-start | bytes 5505028
  74.8 6.1 %collective-permute-start = (bf16[16,1,24,3584]{3,2,1,0:T(8,128)(2,1)}, bf16[16,1,24,3584]{3,2,1,0:T(8,128)(2,1)}, u32[]{:S(2)}, u32[]{:S(2)}) collective-permute-start(bf16[16,1,24,3584]{3,2,1,0:T(8,128)(2,1)} %bitcast.3), channel_id=1, source_target_pairs={{0,1},{1,0},{2,3},{3,2},{4,5},{5,4},{6,7},{7,6},{8,9},{9,8},{10,11... | collective-permute-start | bytes 8257544 | tf_op jit(solution)/shard_map/ppermute | solution.py:13
  83.8 3.3 copy-start.2
  83.9 4.1 copy-start.3
  87.9 120.2 %collective-permute-start.1 = (bf16[16,2,24,3584]{3,2,1,0:T(8,128)(2,1)}, bf16[16,2,24,3584]{3,2,1,0:T(8,128)(2,1)}, u32[]{:S(2)}, u32[]{:S(2)}) collective-permute-start(bf16[16,2,24,3584]{3,2,1,0:T(8,128)(2,1)} %pad_maximum_fusion.1), channel_id=1, source_target_pairs={{0,2},{1,3},{2,0},{3,1},{4,6},{5,7},{6,4},{7,5},{8,10},{9,11},{10,... | collective-permute-start | bytes 16515080 | tf_op jit(solution)/shard_map/ppermute | solution.py:13
  212.8 5.1 copy-start.8
  213.9 4.0 copy-start.4
  239.5 7.5 %copy-start.7 = (s32[128,2]{0,1:T(2,128)S(1)}, s32[128,2]{0,1:T(2,128)}, u32[]{:S(2)}) copy-start(s32[128,2]{0,1:T(2,128)} %param.13) | copy-start | bytes 3076
  239.5 7.9 %copy-start.5 = (bf16[128,3584]{1,0:T(8,128)(2,1)S(1)}, bf16[128,3584]{1,0:T(8,128)(2,1)}, u32[]{:S(2)}) copy-start(bf16[128,3584]{1,0:T(8,128)(2,1)} %param.7) | copy-start | bytes 2752516
  239.5 7.9 %copy-start.6 = (f32[3584]{0:T(1024)S(1)}, f32[3584]{0:T(1024)}, u32[]{:S(2)}) copy-start(f32[3584]{0:T(1024)} %param.8) | copy-start | bytes 43012
  239.6 7.9 %copy-start.9 = (bf16[3584,4]{0,1:T(4,128)(2,1)S(1)}, bf16[3584,4]{0,1:T(4,128)(2,1)}, u32[]{:S(2)}) copy-start(bf16[3584,4]{0,1:T(4,128)(2,1)} %param.9) | copy-start | bytes 86020
  239.6 245.6 %all-to-all-start.1 = ((bf16[16,96,3584]{2,1,0:T(8,128)(2,1)}), bf16[16,96,3584]{2,1,0:T(8,128)(2,1)}, u32[]{:S(2)}, u32[]{:S(2)}) async-start(bf16[16,96,3584]{2,1,0:T(8,128)(2,1)} %bitcast.39), calls=%async_computation.1 | async-start | bytes 22020096 | tf_op jit(solution)/shard_map/all_to_all | solution.py:63
  507.2 10.1 %copy-start.1 = (bf16[256,3584]{1,0:T(8,128)(2,1)S(1)}, bf16[256,3584]{1,0:T(8,128)(2,1)}, u32[]{:S(2)}) copy-start(bf16[256,3584]{1,0:T(8,128)(2,1)} %param.12) | copy-start | bytes 5505028
where the time goes:
time: 518 us; the launch traced here: 517 us
  waiting for transfers between devices  362 us (70%)
  blocking collectives  67.3 us (13%)
  other arithmetic  34.5 us (7%)
  matrix products  24.2 us (5%)
  local copies, waits for them, and re-layouts  20.4 us (4%)
  starting transfers between devices  8.49 us (2%)
    all_to_all x1, waiting for transfers between devices, shards(): lax.all_to_all(partials, 'expert', split_axis=0, concat_axis=0, tiled=True)  237 us
    ppermute x2, waiting for transfers between devices, swapped(): return lax.ppermute(value, axis, pairs)  125 us
    all_to_all x1, blocking collectives, shards(): lax.all_to_all(outgoing, 'expert', split_axis=0, concat_axis=0, tiled=True)  67.3 us
    dot_general x1, matrix products, shards(): jnp.dot(activated, w_down, preferred_element_type=jnp.float32)  17.4 us
    gather x2, local copies, waits for them, and re-layouts, shards(): jnp.take(flat_sums, target, axis=0)  13.3 us
  transfers between devices with their start and end apart: 3, of which 3 were waited for; matrix products, arithmetic and copies ran while one was open for 0% of the time, Pallas kernels for 0%

commit v1 on v0

v1 whole, which is shorter than its diff:
```python
import functools

import jax
import jax.numpy as jnp
from jax import lax
from jax.experimental import pallas as pl
from jax.experimental.pallas import tpu as pltpu
from jax.sharding import PartitionSpec as P

route_scale = 2.5
norm_eps = 1e-06
LANES = 128
MESH = pl.DeviceIdType.MESH

TOK_PIECES = 2
OUT_PIECES = 2
W_PIECES = 4


def kernel(
    groups,
    experts,
    span,
    res_ref,
    gain_ref,
    router_ref,
    ids_ref,
    wg_in,
    wu_in,
    wd_in,
    out_ref,
    tok,
    gates,
    act,
    rx,
    wg,
    wu,
    wd,
    own_sem,
    tok_recv,
    tok_up,
    tok_dn,
    gate_recv,
    gate_up,
    gate_dn,
    ret_send,
    ret_recv,
    y_send,
    y_recv,
    x_send,
    x_recv,
    c_send,
    c_recv,
    cy_send,
    cy_recv,
    cx_send,
    cx_recv,
):
    rows, width = res_ref.shape
    hid = wg_in.shape[1]
    grp = lax.axis_index("groups")
    pos = lax.axis_index("expert")
    exp = pos // span
    mem = pos % span
    last = experts - 1
    has_up = exp < last
    has_dn = exp > 0
    base = exp * span
    mem_y = (mem + 2) % 4
    mem_c = mem + 1 - 2 * (mem % 2)
    mem_yc = (mem_c + 2) % 4
    up = {"groups": grp, "expert": jnp.minimum(pos + span, experts * span - 1)}
    dn = {"groups": grp, "expert": jnp.maximum(pos - span, 0)}
    to_y = {"groups": grp, "expert": base + mem_y}
    to_c = {"groups": grp, "expert": base + mem_c}

    def other(i):
        return (grp + 1 + i) % groups

    barrier = pltpu.get_barrier_semaphore()

    def greet(device):
        pl.semaphore_signal(barrier, inc=1, device_id=device, device_id_type=MESH)

    greet(to_y)
    greet(to_c)
    for i in range(groups - 1):
        greet({"groups": other(i), "expert": pos})

    @pl.when(has_up)
    def _():
        greet(up)

    @pl.when(has_dn)
    def _():
        greet(dn)

    peers = 1 + groups + has_up.astype(jnp.int32) + has_dn.astype(jnp.int32)
    pl.semaphore_wait(barrier, peers)

    mats = ((wg_in, wg), (wu_in, wu), (wd_in, wd))

    def piece(mat, group, index):
        total = mats[mat][0].shape[0]
        size = total // groups // W_PIECES
        return pl.ds(pl.multiple_of(group * (total // groups) + index * size, size), size)

    def remote(src, dst, send, recv, device):
        return pltpu.make_async_remote_copy(
            src_ref=src, dst_ref=dst, send_sem=send, recv_sem=recv, device_id=device, device_id_type=MESH
        )

    def y_copy(mat, index, landing):
        part = piece(mat, grp, index)
        at = mat * W_PIECES + index
        slot = mem_y if landing else mem
        return remote(mats[mat][0].at[part], mats[mat][1].at[slot, part], y_send.at[at], y_recv.at[at], to_y)

    def x_copy(mat, index, i, landing):
        at = mat * W_PIECES + index
        group = (grp + groups - 1 - i) % groups if landing else grp
        part = piece(mat, group, index)
        ref = mats[mat][1].at[mem_y, part]
        return remote(ref, ref, x_send.at[i, at], x_recv.at[i, at], {"groups": other(i), "expert": pos})

    def cy_copy(mat, index, landing):
        at = mat * W_PIECES + index
        part = piece(mat, grp, index)
        ref = mats[mat][1].at[mem_yc if landing else mem_y, part]
        return remote(ref, ref, cy_send.at[at], cy_recv.at[at], to_c)

    def cx_copy(mat, index, i, landing):
        at = mat * W_PIECES + index
        part = piece(mat, (grp + groups - 1 - i) % groups, index)
        ref = mats[mat][1].at[mem_yc if landing else mem_y, part]
        return remote(ref, ref, cx_send.at[i, at], cx_recv.at[i, at], to_c)

    def c_copy(mat, landing):
        slot = mem_c if landing else mem
        return remote(mats[mat][0], mats[mat][1].at[slot], c_send.at[mat], c_recv.at[mat], to_c)

    for mat in range(3):
        for index in range(W_PIECES):
            y_copy(mat, index, False).start()
    own_copies = [pltpu.make_async_copy(mats[i][0], mats[i][1].at[mem], own_sem.at[i]) for i in range(3)]
    for mat in range(3):
        c_copy(mat, False).start()
        own_copies[mat].start()

    step_rows = 16

    def norm_rows(i, carry):
        at = pl.ds(pl.multiple_of(i * step_rows, step_rows), step_rows)
        wide = res_ref[at, :].astype(jnp.float32)
        mean = jnp.mean(wide * wide, axis=1, keepdims=True)
        tok[exp, at, :] = (wide * lax.rsqrt(mean + norm_eps) * gain_ref[...]).astype(jnp.bfloat16)
        return carry

    lax.fori_loop(0, rows // step_rows, norm_rows, 0)
    piece_rows = rows // TOK_PIECES

    def tok_copy(block, index, upward):
        ref = tok.at[block, pl.ds(index * piece_rows, piece_rows)]
        send = (tok_up if upward else tok_dn).at[block, index]
        return remote(ref, ref, send, tok_recv.at[block, index], up if upward else dn)

    def gate_copy(block, upward):
        ref = gates.at[block]
        send = (gate_up if upward else gate_dn).at[block]
        return remote(ref, ref, send, gate_recv.at[block], up if upward else dn)

    def send_block(block, index, upward):
        tok_copy(block, index, upward).start()
        if index == 0:
            gate_copy(block, upward).start()

    def gate_values():
        logits = jnp.dot(tok[exp], router_ref[...], preferred_element_type=jnp.float32)
        affinity = jax.nn.sigmoid(logits)
        lane = lax.broadcasted_iota(jnp.int32, (rows, LANES), 1)
        total = jnp.zeros((rows, 1), jnp.float32)
        spread = jnp.zeros((rows, LANES), jnp.float32)
        for k in range(ids_ref.shape[1]):
            chosen = jnp.where(lane == ids_ref[:, k : k + 1], affinity, 0.0)
            total = total + jnp.sum(chosen, axis=1, keepdims=True)
            spread = spread + chosen
        values = route_scale * spread / total
        gates[exp] = values.T[: gates.shape[1]]

    gate_values()

    @pl.when(has_up)
    def _():
        for index in range(TOK_PIECES):
            send_block(exp, index, True)

    @pl.when(has_dn)
    def _():
        for index in range(TOK_PIECES):
            send_block(exp, index, False)

    def weight_tick(mat, index):
        y_copy(mat, index, True).wait_recv()
        for i in range(groups - 1):
            x_copy(mat, index, i, False).start()
        cy_copy(mat, index, False).start()

    def weight_late(mat, index):
        for i in range(groups - 1):
            x_copy(mat, index, i, True).wait_recv()
            cx_copy(mat, index, i, False).start()

    def token_tick(step, index):
        low = exp - step
        high = exp + step

        @pl.when(low >= 0)
        def _():
            tok_copy(jnp.maximum(low, 0), index, True).wait_recv()
            if index == 0:
                gate_copy(jnp.maximum(low, 0), True).wait_recv()

        @pl.when(jnp.logical_and(low >= 0, has_up))
        def _():
            send_block(jnp.maximum(low, 0), index, True)

        @pl.when(high <= last)
        def _():
            tok_copy(jnp.minimum(high, last), index, False).wait_recv()
            if index == 0:
                gate_copy(jnp.minimum(high, last), False).wait_recv()

        @pl.when(jnp.logical_and(high <= last, has_dn))
        def _():
            send_block(jnp.minimum(high, last), index, False)

    def hidden_part(block, slot):
        rows_in = tok[block]
        gate_proj = jnp.dot(rows_in, wg[slot], preferred_element_type=jnp.float32)
        up_proj = jnp.dot(rows_in, wu[slot], preferred_element_type=jnp.float32)
        sublane = lax.broadcasted_iota(jnp.int32, (gates.shape[1], rows), 0)
        row = jnp.sum(jnp.where(sublane == exp, gates[block], 0.0), axis=0, keepdims=True)
        scale = jnp.broadcast_to(row, (LANES, rows)).T[:, :1]
        hidden = gate_proj / (1.0 + jnp.exp(-gate_proj)) * up_proj * scale
        act[slot, block] = hidden.astype(jnp.bfloat16)

    def hidden_of(block, slots):
        def body(slot, carry):
            hidden_part(block, slot)
            return carry

        lax.fori_loop(0, slots, body, 0)

    def hidden_ready():
        for mat in range(2):
            own_copies[mat].wait()
            c_copy(mat, True).wait_recv()
            for index in range(W_PIECES):
                cy_copy(mat, index, True).wait_recv()
                for i in range(groups - 1):
                    cx_copy(mat, index, i, True).wait_recv()

    events = []
    weight_steps = 3 * W_PIECES
    for tick in range(weight_steps):
        mat, index = divmod(tick, W_PIECES)
        events.append(((tick + 1) / weight_steps, 0, functools.partial(weight_tick, mat, index)))
        events.append(((tick + 2) / weight_steps, 1, functools.partial(weight_late, mat, index)))
    token_steps = last * TOK_PIECES
    for tick in range(token_steps):
        step, index = divmod(tick, TOK_PIECES)
        events.append(((tick + 1) / token_steps, 2, functools.partial(token_tick, step + 1, index)))
    events.sort(key=lambda event: event[:2])
    for event in events:
        event[2]()
    hidden_ready()

    def hidden_body(block, carry):
        hidden_of(block, span)
        return carry

    lax.fori_loop(0, experts, hidden_body, 0)

    own_copies[2].wait()
    c_copy(2, True).wait_recv()
    for index in range(W_PIECES):
        cy_copy(2, index, True).wait_recv()
        for i in range(groups - 1):
            cx_copy(2, index, i, True).wait_recv()

    def sent(block, carry):
        @pl.when(jnp.logical_and(block <= exp, has_up))
        def _():
            for index in range(TOK_PIECES):
                tok_copy(block, index, True).wait_send()
            gate_copy(block, True).wait_send()

        @pl.when(jnp.logical_and(block >= exp, has_dn))
        def _():
            for index in range(TOK_PIECES):
                tok_copy(block, index, False).wait_send()
            gate_copy(block, False).wait_send()

        return carry

    lax.fori_loop(0, experts, sent, 0)

    cols = width // OUT_PIECES
    tile = 256

    def out_copy(block, index, upward, landing):
        part = pl.ds(index * cols, cols)
        into = block
        if not upward:
            target = exp if landing else exp - 1
            into = jnp.where(block == target, experts, block)
        return remote(
            tok.at[block, :, part],
            rx.at[into, :, part],
            ret_send.at[block, index],
            ret_recv.at[into, index],
            up if upward else dn,
        )

    def share(block, at):
        total = jnp.dot(act[0, block], wd[0, :, at], preferred_element_type=jnp.float32)
        for slot in range(1, span):
            total = total + jnp.dot(act[slot, block], wd[slot, :, at], preferred_element_type=jnp.float32)
        return total

    def send_result(block, upward):
        joins = (exp > 0) if upward else (exp < last)
        for index in range(OUT_PIECES):

            @pl.when(joins)
            def _():
                out_copy(block, index, upward, True).wait_recv()

                def body(i, carry):
                    at = pl.ds(pl.multiple_of(index * cols + i * tile, tile), tile)
                    total = share(block, at) + rx[block, :, at].astype(jnp.float32)
                    tok[block, :, at] = total.astype(jnp.bfloat16)
                    return carry

                lax.fori_loop(0, cols // tile, body, 0)

            @pl.when(jnp.logical_not(joins))
            def _():
                def body(i, carry):
                    at = pl.ds(pl.multiple_of(index * cols + i * tile, tile), tile)
                    tok[block, :, at] = share(block, at).astype(jnp.bfloat16)
                    return carry

                lax.fori_loop(0, cols // tile, body, 0)

            out_copy(block, index, upward, False).start()

    def return_step(step, carry):
        low = exp - (experts - step)
        high = exp + (experts - step)

        @pl.when(low >= 0)
        def _():
            send_result(jnp.maximum(low, 0), False)

        @pl.when(high <= last)
        def _():
            send_result(jnp.minimum(high, last), True)

        return carry

    lax.fori_loop(1, experts, return_step, 0)

    def finish(index):
        @pl.when(has_dn)
        def _():
            out_copy(exp, index, True, True).wait_recv()

        @pl.when(has_up)
        def _():
            out_copy(exp, index, False, True).wait_recv()

        def body(i, carry):
            at = pl.ds(pl.multiple_of(index * cols + i * tile, tile), tile)
            total = res_ref[:, at].astype(jnp.float32) + share(exp, at)
            below = jnp.where(has_dn, rx[exp, :, at].astype(jnp.float32), 0.0)
            above = jnp.where(has_up, rx[experts, :, at].astype(jnp.float32), 0.0)
            out_ref[:, at] = (total + below + above).astype(jnp.bfloat16)
            return carry

        lax.fori_loop(0, cols // tile, body, 0)

    for index in range(OUT_PIECES):
        finish(index)

    def results_sent(block, carry):
        @pl.when(block < exp)
        def _():
            for index in range(OUT_PIECES):
                out_copy(block, index, False, False).wait_send()

        @pl.when(block > exp)
        def _():
            for index in range(OUT_PIECES):
                out_copy(block, index, True, False).wait_send()

        return carry

    lax.fori_loop(0, experts, results_sent, 0)
    for mat in range(3):
        c_copy(mat, False).wait_send()
        for index in range(W_PIECES):
            y_copy(mat, index, False).wait_send()
            cy_copy(mat, index, False).wait_send()
            for i in range(groups - 1):
                x_copy(mat, index, i, False).wait_send()
                cx_copy(mat, index, i, False).wait_send()


def shards(residual, norm_gain, router, w_gate, w_up, w_down, expert_ids):
    rows, width = residual.shape
    experts = router.shape[1]
    groups = lax.axis_size("groups")
    span = lax.axis_size("expert") // experts
    assert span == 4
    hid = w_gate.shape[1]
    gate_rows = max(8, experts)
    wide_router = jnp.pad(router, ((0, 0), (0, LANES - experts)))
    vmem = pl.BlockSpec(memory_space=pltpu.VMEM)
    anywhere = pl.BlockSpec(memory_space=pl.ANY)
    dma = pltpu.SemaphoreType.DMA
    weight_copies = 3 * W_PIECES
    return pl.pallas_call(
        functools.partial(kernel, groups, experts, span),
        out_shape=jax.ShapeDtypeStruct((rows, width), jnp.bfloat16),
        in_specs=[vmem, vmem, vmem, vmem, anywhere, anywhere, anywhere],
        out_specs=vmem,
        scratch_shapes=[
            pltpu.VMEM((experts, rows, width), jnp.bfloat16),
            pltpu.VMEM((experts, gate_rows, rows), jnp.float32),
            pltpu.VMEM((span, experts, rows, hid), jnp.bfloat16),
            pltpu.VMEM((experts + 1, rows, width), jnp.bfloat16),
            pltpu.VMEM((span, width, hid), jnp.bfloat16),
            pltpu.VMEM((span, width, hid), jnp.bfloat16),
            pltpu.VMEM((span, hid, width), jnp.bfloat16),
            dma((3,)),
            dma((experts, TOK_PIECES)),
            dma((experts, TOK_PIECES)),
            dma((experts, TOK_PIECES)),
            dma((experts,)),
            dma((experts,)),
            dma((experts,)),
            dma((experts, OUT_PIECES)),
            dma((experts + 1, OUT_PIECES)),
            dma((weight_copies,)),
            dma((weight_copies,)),
            dma((groups - 1, weight_copies)),
            dma((groups - 1, weight_copies)),
            dma((3,)),
            dma((3,)),
            dma((weight_copies,)),
            dma((weight_copies,)),
            dma((groups - 1, weight_copies)),
            dma((groups - 1, weight_copies)),
        ],
        compiler_params=pltpu.CompilerParams(
            collective_id=0, has_side_effects=True, vmem_limit_bytes=67043328
        ),
    )(residual, norm_gain.reshape(1, width), wide_router, expert_ids, w_gate, w_up, w_down)


def solution(mesh):
    in_specs = (
        P(("groups", "expert"), None),
        P(),
        P(),
        P(None, "expert"),
        P(None, "expert"),
        P("expert", None),
        P(("groups", "expert"), None),
    )
    out_specs = P(("groups", "expert"), None)
    return jax.shard_map(shards, mesh=mesh, in_specs=in_specs, out_specs=out_specs, check_vma=False)
```

time: 518 us -> 158 us (0.31)
  the two profiles are of different devices: /device:TPU:17 before, /device:TPU:24 now
where the time goes in v1:
time: 158 us; the launch traced here: 157 us
  Pallas kernels  150 us (95%)
  local copies, waits for them, and re-layouts  7.3 us (5%)
    pallas_call x1, Pallas kernels, shards(): pl.pallas_call(functools.partial(kernel, groups, experts, span), out_shap...  150 us
    unnamed x3, local copies, waits for them, and re-layouts  4.87 us

profile of v1, /device:TPU:24, one launch (start us, length us, event | category | flops | bytes accessed | tf_op | source)
XLA Modules:
  0.0 157.3 jit_solution(262454002263106803)
XLA Ops:
  0.0 1.3 reshape.3.gain_ref
  1.3 1.4 copy.9.ids_ref
  2.7 1.3 copy.8
  4.0 1.1 pad.4.router_ref
  5.2 150.0 %shard_map.73 = bf16[128,3584]{1,0:T(8,128)(2,1)} custom-call(bf16[128,3584]{1,0:T(8,128)(2,1)} %res_ref.1, f32[1,3584]{1,0:T(1,128)} %reshape.3.gain_ref, bf16[3584,128]{1,0:T(8,128)(2,1)} %pad.4.router_ref, s32[128,2]{1,0:T(8,128)} %copy.9.ids_ref, bf16[3584,256]{1,0:T(8,128)(2,1)} %wg_in.1, bf16[3584,256]{1,0:T(8,128)(2,1)} %wu_in.1, bf16[256,3584]{1,0:T(8,128)(2,1)} %wd_in.1), custom_call_target="tpu_custom_call" | custom-call | tf_op jit(solution)/shard_map/pallas_call | solution.py:433
  155.2 2.2 %copy.11 = bf16[128,3584]{1,0:T(8,128)(2,1)} copy(bf16[128,3584]{1,0:T(8,128)(2,1)} %shard_map.73) | data formatting | bytes 1835008

commit v2 on v1

--- a/solution.py
+++ b/solution.py
@@ -21,6 +21,7 @@
     groups,
     experts,
     span,
+    capacity,
     res_ref,
     gain_ref,
     router_ref,
@@ -33,6 +34,7 @@
     gates,
     act,
     rx,
+    acc,
     wg,
     wu,
     wd,
@@ -153,7 +155,7 @@
         at = pl.ds(pl.multiple_of(i * step_rows, step_rows), step_rows)
         wide = res_ref[at, :].astype(jnp.float32)
         mean = jnp.mean(wide * wide, axis=1, keepdims=True)
-        tok[exp, at, :] = (wide * lax.rsqrt(mean + norm_eps) * gain_ref[...]).astype(jnp.bfloat16)
+        tok[exp, at, :] = (wide * lax.rsqrt(mean + norm_eps) * gain_ref[...].reshape(1, width)).astype(jnp.bfloat16)
         return carry
 
     lax.fori_loop(0, rows // step_rows, norm_rows, 0)
@@ -175,17 +177,15 @@
             gate_copy(block, upward).start()
 
     def gate_values():
-        logits = jnp.dot(tok[exp], router_ref[...], preferred_element_type=jnp.float32)
+        logits = lax.dot_general(
+            router_ref[...], tok[exp], (((1,), (1,)), ((), ())), preferred_element_type=jnp.float32
+        )
         affinity = jax.nn.sigmoid(logits)
-        lane = lax.broadcasted_iota(jnp.int32, (rows, LANES), 1)
-        total = jnp.zeros((rows, 1), jnp.float32)
-        spread = jnp.zeros((rows, LANES), jnp.float32)
-        for k in range(ids_ref.shape[1]):
-            chosen = jnp.where(lane == ids_ref[:, k : k + 1], affinity, 0.0)
-            total = total + jnp.sum(chosen, axis=1, keepdims=True)
-            spread = spread + chosen
-        values = route_scale * spread / total
-        gates[exp] = values.T[: gates.shape[1]]
+        expert = lax.broadcasted_iota(jnp.int32, (experts, rows), 0)
+        spread = jnp.zeros((experts, rows), jnp.float32)
+        for k in range(ids_ref.shape[0]):
+            spread = spread + jnp.where(expert == ids_ref[k : k + 1, :], affinity, 0.0)
+        gates[exp] = route_scale * spread / jnp.sum(spread, axis=0, keepdims=True)
 
     gate_values()
 
@@ -244,21 +244,32 @@
         hidden = gate_proj / (1.0 + jnp.exp(-gate_proj)) * up_proj * scale
         act[slot, block] = hidden.astype(jnp.bfloat16)
 
-    def hidden_of(block, slots):
-        def body(slot, carry):
-            hidden_part(block, slot)
-            return carry
-
-        lax.fori_loop(0, slots, body, 0)
-
-    def hidden_ready():
+    def first_slices():
         for mat in range(2):
             own_copies[mat].wait()
             c_copy(mat, True).wait_recv()
+
+    def all_slices():
+        for mat in range(2):
             for index in range(W_PIECES):
                 cy_copy(mat, index, True).wait_recv()
                 for i in range(groups - 1):
                     cx_copy(mat, index, i, True).wait_recv()
+
+    def hidden_step(step, first, second, count=2):
+        def body(i, carry):
+            side = i // count
+            turn = i % count
+            block = exp - step + 2 * step * side
+            slot = jnp.where(turn == 0, first, jnp.where(turn == 1, second, jnp.where(turn == 2, mem_y, mem_yc)))
+
+            @pl.when(jnp.logical_and(block >= 0, block <= last))
+            def _():
+                hidden_part(jnp.clip(block, 0, last), slot)
+
+            return carry
+
+        lax.fori_loop(0, count if step == 0 else 2 * count, body, 0)
 
     events = []
     weight_steps = 3 * W_PIECES
@@ -270,16 +281,20 @@
     for tick in range(token_steps):
         step, index = divmod(tick, TOK_PIECES)
         events.append(((tick + 1) / token_steps, 2, functools.partial(token_tick, step + 1, index)))
+    ready = (2 * W_PIECES + 2) / weight_steps
+    events.append((1.5 / weight_steps, 3, first_slices))
+    events.append((ready, 3, all_slices))
+    for step in range(experts):
+        there = max(step / last, 1.5 / weight_steps)
+        if there >= ready:
+            events.append((there, 4, functools.partial(hidden_step, step, mem, mem_c, span)))
+        else:
+            events.append((there, 4, functools.partial(hidden_step, step, mem, mem_c)))
+            late = ready + 0.4 * step / weight_steps
+            events.append((late, 4, functools.partial(hidden_step, step, mem_y, mem_yc)))
     events.sort(key=lambda event: event[:2])
     for event in events:
         event[2]()
-    hidden_ready()
-
-    def hidden_body(block, carry):
-        hidden_of(block, span)
-        return carry
-
-    lax.fori_loop(0, experts, hidden_body, 0)
 
     own_copies[2].wait()
     c_copy(2, True).wait_recv()
@@ -308,101 +323,176 @@
     cols = width // OUT_PIECES
     tile = 256
 
-    def out_copy(block, index, upward, landing):
+    def out_copy(block, index, upward, landing, packed):
         part = pl.ds(index * cols, cols)
+        height = pl.ds(0, capacity if packed else rows)
         into = block
         if not upward:
             target = exp if landing else exp - 1
             into = jnp.where(block == target, experts, block)
         return remote(
-            tok.at[block, :, part],
-            rx.at[into, :, part],
+            tok.at[block, height, part],
+            rx.at[into, height, part],
             ret_send.at[block, index],
             ret_recv.at[into, index],
             up if upward else dn,
         )
 
-    def share(block, at):
-        total = jnp.dot(act[0, block], wd[0, :, at], preferred_element_type=jnp.float32)
+    def share(block, at, height=rows):
+        part = pl.ds(0, height)
+        total = jnp.dot(act[0, block, part], wd[0, :, at], preferred_element_type=jnp.float32)
         for slot in range(1, span):
-            total = total + jnp.dot(act[slot, block], wd[slot, :, at], preferred_element_type=jnp.float32)
+            total = total + jnp.dot(act[slot, block, part], wd[slot, :, at], preferred_element_type=jnp.float32)
         return total
 
-    def send_result(block, upward):
-        joins = (exp > 0) if upward else (exp < last)
-        for index in range(OUT_PIECES):
-
-            @pl.when(joins)
-            def _():
-                out_copy(block, index, upward, True).wait_recv()
-
-                def body(i, carry):
-                    at = pl.ds(pl.multiple_of(index * cols + i * tile, tile), tile)
-                    total = share(block, at) + rx[block, :, at].astype(jnp.float32)
-                    tok[block, :, at] = total.astype(jnp.bfloat16)
-                    return carry
-
-                lax.fori_loop(0, cols // tile, body, 0)
-
-            @pl.when(jnp.logical_not(joins))
-            def _():
-                def body(i, carry):
-                    at = pl.ds(pl.multiple_of(index * cols + i * tile, tile), tile)
-                    tok[block, :, at] = share(block, at).astype(jnp.bfloat16)
-                    return carry
-
-                lax.fori_loop(0, cols // tile, body, 0)
-
-            out_copy(block, index, upward, False).start()
+    def packing(block, expert):
+        sublane = lax.broadcasted_iota(jnp.int32, (gates.shape[1], rows), 0)
+        row = jnp.sum(jnp.where(sublane == expert, gates[block], 0.0), axis=0, keepdims=True)
+        taken = jnp.broadcast_to(jnp.where(row != 0.0, 1.0, 0.0), (capacity, rows))
+        source = lax.broadcasted_iota(jnp.int32, (rows, rows), 0)
+        dest = lax.broadcasted_iota(jnp.int32, (rows, rows), 1)
+        earlier = jnp.where(source < dest, 1.0, 0.0).astype(jnp.bfloat16)
+        rank = jnp.dot(taken.astype(jnp.bfloat16), earlier, preferred_element_type=jnp.float32)
+        slot = lax.broadcasted_iota(jnp.int32, (capacity, rows), 0).astype(jnp.float32)
+        return jnp.where(rank == slot, taken, 0.0).astype(jnp.bfloat16)
+
+    def unpacked(picks, value):
+        return lax.dot_general(picks, value, (((0,), (0,)), ((), ())), preferred_element_type=jnp.float32)
+
+    def tiles_of(index, body):
+        def run(i, carry):
+            body(pl.ds(pl.multiple_of(index * cols + i * tile, tile), tile))
+            return carry
+
+        lax.fori_loop(0, cols // tile, run, 0)
+
+    def neighbour(upward):
+        return exp - 1 if upward else exp + 1
+
+    def is_end(expert, upward):
+        return expert == (0 if upward else last)
+
+    def send_result(block, index, upward):
+        first = is_end(exp, upward)
+        second = is_end(neighbour(upward), upward)
+
+        @pl.when(first)
+        def _():
+            if index == 0:
+                picks = packing(block, exp)
+                for slot in range(span):
+                    act[slot, block, pl.ds(0, capacity)] = jnp.dot(
+                        picks, act[slot, block], preferred_element_type=jnp.float32
+                    ).astype(jnp.bfloat16)
+
+            def body(at):
+                tok[block, pl.ds(0, capacity), at] = share(block, at, capacity).astype(jnp.bfloat16)
+
+            tiles_of(index, body)
+            out_copy(block, index, upward, False, True).start()
+
+        @pl.when(second)
+        def _():
+            out_copy(block, index, upward, True, True).wait_recv()
+            picks = packing(block, neighbour(upward))
+
+            def body(at):
+                total = share(block, at) + unpacked(picks, rx[block, pl.ds(0, capacity), at])
+                tok[block, :, at] = total.astype(jnp.bfloat16)
+
+            tiles_of(index, body)
+
+        @pl.when(jnp.logical_not(jnp.logical_or(first, second)))
+        def _():
+            out_copy(block, index, upward, True, False).wait_recv()
+
+            def body(at):
+                total = share(block, at) + rx[block, :, at].astype(jnp.float32)
+                tok[block, :, at] = total.astype(jnp.bfloat16)
+
+            tiles_of(index, body)
+
+        @pl.when(jnp.logical_not(first))
+        def _():
+            out_copy(block, index, upward, False, False).start()
 
     def return_step(step, carry):
         low = exp - (experts - step)
         high = exp + (experts - step)
-
-        @pl.when(low >= 0)
-        def _():
-            send_result(jnp.maximum(low, 0), False)
-
-        @pl.when(high <= last)
-        def _():
-            send_result(jnp.minimum(high, last), True)
+        for index in range(OUT_PIECES):
+
+            @pl.when(low >= 0)
+            def _():
+                send_result(jnp.maximum(low, 0), index, False)
+
+            @pl.when(high <= last)
+            def _():
+                send_result(jnp.minimum(high, last), index, True)
 
         return carry
 
     lax.fori_loop(1, experts, return_step, 0)
 
-    def finish(index):
-        @pl.when(has_dn)
-        def _():
-            out_copy(exp, index, True, True).wait_recv()
-
-        @pl.when(has_up)
-        def _():
-            out_copy(exp, index, False, True).wait_recv()
-
-        def body(i, carry):
-            at = pl.ds(pl.multiple_of(index * cols + i * tile, tile), tile)
-            total = res_ref[:, at].astype(jnp.float32) + share(exp, at)
-            below = jnp.where(has_dn, rx[exp, :, at].astype(jnp.float32), 0.0)
-            above = jnp.where(has_up, rx[experts, :, at].astype(jnp.float32), 0.0)
-            out_ref[:, at] = (total + below + above).astype(jnp.bfloat16)
-            return carry
-
-        lax.fori_loop(0, cols // tile, body, 0)
+    def own_body(i, carry):
+        at = pl.ds(pl.multiple_of(i * tile, tile), tile)
+        acc[:, at] = res_ref[:, at].astype(jnp.float32) + share(exp, at)
+        return carry
+
+    lax.fori_loop(0, width // tile, own_body, 0)
+
+    def join(index, upward):
+        slot = exp if upward else experts
+        second = is_end(neighbour(upward), upward)
+
+        @pl.when(second)
+        def _():
+            out_copy(exp, index, upward, True, True).wait_recv()
+            picks = packing(exp, neighbour(upward))
+
+            def body(at):
+                acc[:, at] += unpacked(picks, rx[slot, pl.ds(0, capacity), at])
+
+            tiles_of(index, body)
+
+        @pl.when(jnp.logical_not(jnp.logical_or(second, is_end(exp, upward))))
+        def _():
+            out_copy(exp, index, upward, True, False).wait_recv()
+
+            def body(at):
+                acc[:, at] += rx[slot, :, at].astype(jnp.float32)
+
+            tiles_of(index, body)
 
     for index in range(OUT_PIECES):
-        finish(index)
+        join(index, True)
+        join(index, False)
+
+        def write(at):
+            out_ref[:, at] = acc[:, at].astype(jnp.bfloat16)
+
+        tiles_of(index, write)
+
+    def wait_result(block, upward):
+        first = is_end(exp, upward)
+
+        @pl.when(first)
+        def _():
+            for index in range(OUT_PIECES):
+                out_copy(block, index, upward, False, True).wait_send()
+
+        @pl.when(jnp.logical_not(first))
+        def _():
+            for index in range(OUT_PIECES):
+                out_copy(block, index, upward, False, False).wait_send()
 
     def results_sent(block, carry):
         @pl.when(block < exp)
         def _():
-            for index in range(OUT_PIECES):
-                out_copy(block, index, False, False).wait_send()
+            wait_result(block, False)
 
         @pl.when(block > exp)
         def _():
-            for index in range(OUT_PIECES):
-                out_copy(block, index, True, False).wait_send()
+            wait_result(block, True)
 
         return carry
 
@@ -424,22 +514,23 @@
     span = lax.axis_size("expert") // experts
     assert span == 4
     hid = w_gate.shape[1]
-    gate_rows = max(8, experts)
-    wide_router = jnp.pad(router, ((0, 0), (0, LANES - experts)))
+    capacity = 3 * rows * expert_ids.shape[1] // (2 * experts)
+    capacity = min(rows, -(-capacity // 16) * 16)
     vmem = pl.BlockSpec(memory_space=pltpu.VMEM)
     anywhere = pl.BlockSpec(memory_space=pl.ANY)
     dma = pltpu.SemaphoreType.DMA
     weight_copies = 3 * W_PIECES
     return pl.pallas_call(
-        functools.partial(kernel, groups, experts, span),
+        functools.partial(kernel, groups, experts, span, capacity),
         out_shape=jax.ShapeDtypeStruct((rows, width), jnp.bfloat16),
         in_specs=[vmem, vmem, vmem, vmem, anywhere, anywhere, anywhere],
         out_specs=vmem,
         scratch_shapes=[
             pltpu.VMEM((experts, rows, width), jnp.bfloat16),
-            pltpu.VMEM((experts, gate_rows, rows), jnp.float32),
+            pltpu.VMEM((experts, experts, rows), jnp.float32),
             pltpu.VMEM((span, experts, rows, hid), jnp.bfloat16),
             pltpu.VMEM((experts + 1, rows, width), jnp.bfloat16),
+            pltpu.VMEM((rows, width), jnp.float32),
             pltpu.VMEM((span, width, hid), jnp.bfloat16),
             pltpu.VMEM((span, width, hid), jnp.bfloat16),
             pltpu.VMEM((span, hid, width), jnp.bfloat16),
@@ -466,7 +557,7 @@
         compiler_params=pltpu.CompilerParams(
             collective_id=0, has_side_effects=True, vmem_limit_bytes=67043328
         ),
-    )(residual, norm_gain.reshape(1, width), wide_router, expert_ids, w_gate, w_up, w_down)
+    )(residual, norm_gain, router.T, expert_ids.T, w_gate, w_up, w_down)
 
 
 def solution(mesh):

time: 158 us -> 132 us (0.84)
  the two profiles are of different devices: /device:TPU:24 before, /device:TPU:17 now
where the time goes in v2:
time: 132 us
  Pallas kernels  129 us (98%)
  local copies, waits for them, and re-layouts  2.16 us (2%)
    pallas_call x1, Pallas kernels, shards(): pl.pallas_call(functools.partial(kernel, groups, experts, span, capacity)...  129 us

profile of v2, /device:TPU:17, one launch (start us, length us, event | category | flops | bytes accessed | tf_op | source)
XLA Modules:
  0.0 131.6 jit_solution(3590797556090630602)
XLA Ops:
  0.0 129.4 %shard_map.73 = bf16[128,3584]{1,0:T(8,128)(2,1)} custom-call(bf16[128,3584]{1,0:T(8,128)(2,1)} %res_ref.1, f32[3584]{0:T(1024)} %gain_ref.1, bf16[4,3584]{1,0:T(4,128)(2,1)} %bitcast.2, s32[2,128]{1,0:T(2,128)} %bitcast.3, bf16[3584,256]{1,0:T(8,128)(2,1)} %wg_in.1, bf16[3584,256]{1,0:T(8,128)(2,1)} %wu_in.1, bf16[256,3584]{1,0:T(8,128)(2,1)} %wd_in.1), custom_call_target="tpu_custom_call" | custom-call | tf_op jit(solution)/shard_map/pallas_call | solution.py:523
  129.4 2.2 %copy.9 = bf16[128,3584]{1,0:T(8,128)(2,1)} copy(bf16[128,3584]{1,0:T(8,128)(2,1)} %shard_map.73) | data formatting | bytes 1835008

commit v3 on v2

--- a/solution.py
+++ b/solution.py
@@ -13,8 +13,8 @@
 MESH = pl.DeviceIdType.MESH
 
 TOK_PIECES = 2
-OUT_PIECES = 2
-W_PIECES = 4
+OUT_PIECES = 7
+W_PIECES = (4, 4, 7)
 
 
 def kernel(
@@ -102,10 +102,14 @@
 
     mats = ((wg_in, wg), (wu_in, wu), (wd_in, wd))
 
-    def piece(mat, group, index):
-        total = mats[mat][0].shape[0]
-        size = total // groups // W_PIECES
-        return pl.ds(pl.multiple_of(group * (total // groups) + index * size, size), size)
+    def piece(ref, mat, group, index):
+        total = mats[mat][0].shape[mat // 2]
+        size = total // groups // W_PIECES[mat]
+        part = pl.ds(pl.multiple_of(group * (total // groups) + index * size, size), size)
+        return ref.at[:, part] if mat == 2 else ref.at[part]
+
+    def number(mat, index):
+        return sum(W_PIECES[:mat]) + index
 
     def remote(src, dst, send, recv, device):
         return pltpu.make_async_remote_copy(
@@ -113,28 +117,25 @@
         )
 
     def y_copy(mat, index, landing):
-        part = piece(mat, grp, index)
-        at = mat * W_PIECES + index
-        slot = mem_y if landing else mem
-        return remote(mats[mat][0].at[part], mats[mat][1].at[slot, part], y_send.at[at], y_recv.at[at], to_y)
+        at = number(mat, index)
+        into = piece(mats[mat][1].at[mem_y if landing else mem], mat, grp, index)
+        return remote(piece(mats[mat][0], mat, grp, index), into, y_send.at[at], y_recv.at[at], to_y)
 
     def x_copy(mat, index, i, landing):
-        at = mat * W_PIECES + index
+        at = number(mat, index)
         group = (grp + groups - 1 - i) % groups if landing else grp
-        part = piece(mat, group, index)
-        ref = mats[mat][1].at[mem_y, part]
+        ref = piece(mats[mat][1].at[mem_y], mat, group, index)
         return remote(ref, ref, x_send.at[i, at], x_recv.at[i, at], {"groups": other(i), "expert": pos})
 
     def cy_copy(mat, index, landing):
-        at = mat * W_PIECES + index
-        part = piece(mat, grp, index)
-        ref = mats[mat][1].at[mem_yc if landing else mem_y, part]
+        at = number(mat, index)
+        ref = piece(mats[mat][1].at[mem_yc if landing else mem_y], mat, grp, index)
         return remote(ref, ref, cy_send.at[at], cy_recv.at[at], to_c)
 
     def cx_copy(mat, index, i, landing):
-        at = mat * W_PIECES + index
-        part = piece(mat, (grp + groups - 1 - i) % groups, index)
-        ref = mats[mat][1].at[mem_yc if landing else mem_y, part]
+        at = number(mat, index)
+        group = (grp + groups - 1 - i) % groups
+        ref = piece(mats[mat][1].at[mem_yc if landing else mem_y], mat, group, index)
         return remote(ref, ref, cx_send.at[i, at], cx_recv.at[i, at], to_c)
 
     def c_copy(mat, landing):
@@ -142,7 +143,7 @@
         return remote(mats[mat][0], mats[mat][1].at[slot], c_send.at[mat], c_recv.at[mat], to_c)
 
     for mat in range(3):
-        for index in range(W_PIECES):
+        for index in range(W_PIECES[mat]):
             y_copy(mat, index, False).start()
     own_copies = [pltpu.make_async_copy(mats[i][0], mats[i][1].at[mem], own_sem.at[i]) for i in range(3)]
     for mat in range(3):
@@ -158,7 +159,6 @@
         tok[exp, at, :] = (wide * lax.rsqrt(mean + norm_eps) * gain_ref[...].reshape(1, width)).astype(jnp.bfloat16)
         return carry
 
-    lax.fori_loop(0, rows // step_rows, norm_rows, 0)
     piece_rows = rows // TOK_PIECES
 
     def tok_copy(block, index, upward):
@@ -173,7 +173,7 @@
 
     def send_block(block, index, upward):
         tok_copy(block, index, upward).start()
-        if index == 0:
+        if index == TOK_PIECES - 1:
             gate_copy(block, upward).start()
 
     def gate_values():
@@ -187,17 +187,27 @@
             spread = spread + jnp.where(expert == ids_ref[k : k + 1, :], affinity, 0.0)
         gates[exp] = route_scale * spread / jnp.sum(spread, axis=0, keepdims=True)
 
+    steps = piece_rows // step_rows
+    for index in range(TOK_PIECES):
+        lax.fori_loop(index * steps, (index + 1) * steps, norm_rows, 0)
+
+        @pl.when(has_up)
+        def _():
+            tok_copy(exp, index, True).start()
+
+        @pl.when(has_dn)
+        def _():
+            tok_copy(exp, index, False).start()
+
     gate_values()
 
     @pl.when(has_up)
     def _():
-        for index in range(TOK_PIECES):
-            send_block(exp, index, True)
+        gate_copy(exp, True).start()
 
     @pl.when(has_dn)
     def _():
-        for index in range(TOK_PIECES):
-            send_block(exp, index, False)
+        gate_copy(exp, False).start()
 
     def weight_tick(mat, index):
         y_copy(mat, index, True).wait_recv()
@@ -217,7 +227,7 @@
         @pl.when(low >= 0)
         def _():
             tok_copy(jnp.maximum(low, 0), index, True).wait_recv()
-            if index == 0:
+            if index == TOK_PIECES - 1:
                 gate_copy(jnp.maximum(low, 0), True).wait_recv()
 
         @pl.when(jnp.logical_and(low >= 0, has_up))
@@ -227,7 +237,7 @@
         @pl.when(high <= last)
         def _():
             tok_copy(jnp.minimum(high, last), index, False).wait_recv()
-            if index == 0:
+            if index == TOK_PIECES - 1:
                 gate_copy(jnp.minimum(high, last), False).wait_recv()
 
         @pl.when(jnp.logical_and(high <= last, has_dn))
@@ -251,7 +261,7 @@
 
     def all_slices():
         for mat in range(2):
-            for index in range(W_PIECES):
+            for index in range(W_PIECES[mat]):
                 cy_copy(mat, index, True).wait_recv()
                 for i in range(groups - 1):
                     cx_copy(mat, index, i, True).wait_recv()
@@ -272,25 +282,26 @@
         lax.fori_loop(0, count if step == 0 else 2 * count, body, 0)
 
     events = []
-    weight_steps = 3 * W_PIECES
-    for tick in range(weight_steps):
-        mat, index = divmod(tick, W_PIECES)
-        events.append(((tick + 1) / weight_steps, 0, functools.partial(weight_tick, mat, index)))
-        events.append(((tick + 2) / weight_steps, 1, functools.partial(weight_late, mat, index)))
+    for mat in range(3):
+        for index in range(W_PIECES[mat]):
+            size = 1 / 3 / W_PIECES[mat]
+            when = mat / 3 + (index + 1) * size
+            events.append((when, 0, functools.partial(weight_tick, mat, index)))
+            events.append((when + size, 1, functools.partial(weight_late, mat, index)))
     token_steps = last * TOK_PIECES
     for tick in range(token_steps):
         step, index = divmod(tick, TOK_PIECES)
         events.append(((tick + 1) / token_steps, 2, functools.partial(token_tick, step + 1, index)))
-    ready = (2 * W_PIECES + 2) / weight_steps
-    events.append((1.5 / weight_steps, 3, first_slices))
+    ready = 0.83
+    events.append((0.12, 3, first_slices))
     events.append((ready, 3, all_slices))
     for step in range(experts):
-        there = max(step / last, 1.5 / weight_steps)
+        there = max(step / last, 0.12)
         if there >= ready:
             events.append((there, 4, functools.partial(hidden_step, step, mem, mem_c, span)))
         else:
             events.append((there, 4, functools.partial(hidden_step, step, mem, mem_c)))
-            late = ready + 0.4 * step / weight_steps
+            late = ready + 0.04 * step
             events.append((late, 4, functools.partial(hidden_step, step, mem_y, mem_yc)))
     events.sort(key=lambda event: event[:2])
     for event in events:
@@ -298,7 +309,7 @@
 
     own_copies[2].wait()
     c_copy(2, True).wait_recv()
-    for index in range(W_PIECES):
+    for index in range(W_PIECES[2]):
         cy_copy(2, index, True).wait_recv()
         for i in range(groups - 1):
             cx_copy(2, index, i, True).wait_recv()
@@ -499,7 +510,7 @@
     lax.fori_loop(0, experts, results_sent, 0)
     for mat in range(3):
         c_copy(mat, False).wait_send()
-        for index in range(W_PIECES):
+        for index in range(W_PIECES[mat]):
             y_copy(mat, index, False).wait_send()
             cy_copy(mat, index, False).wait_send()
             for i in range(groups - 1):
@@ -519,7 +530,7 @@
     vmem = pl.BlockSpec(memory_space=pltpu.VMEM)
     anywhere = pl.BlockSpec(memory_space=pl.ANY)
     dma = pltpu.SemaphoreType.DMA
-    weight_copies = 3 * W_PIECES
+    weight_copies = sum(W_PIECES)
     return pl.pallas_call(
         functools.partial(kernel, groups, experts, span, capacity),
         out_shape=jax.ShapeDtypeStruct((rows, width), jnp.bfloat16),

time: 132 us -> 127 us (0.962)
  Pallas kernels: 129 us -> 124 us
    pallas_call x1, Pallas kernels: 129 us -> 124 us  [shards(): pl.pallas_call(functools.partial(kernel, groups, experts, span, capacity)...]
where the time goes in v3:
time: 127 us; the launch traced here: 126 us
  Pallas kernels  124 us (98%)
  local copies, waits for them, and re-layouts  2.16 us (2%)
    pallas_call x1, Pallas kernels, shards(): pl.pallas_call(functools.partial(kernel, groups, experts, span, capacity)...  124 us

profile of v3, /device:TPU:17, one launch (start us, length us, event | category | flops | bytes accessed | tf_op | source)
XLA Modules:
  0.0 126.3 jit_solution(14643582655347468171)
XLA Ops:
  0.0 124.2 %shard_map.73 = bf16[128,3584]{1,0:T(8,128)(2,1)} custom-call(bf16[128,3584]{1,0:T(8,128)(2,1)} %res_ref.1, f32[3584]{0:T(1024)} %gain_ref.1, bf16[4,3584]{1,0:T(4,128)(2,1)} %bitcast.2, s32[2,128]{1,0:T(2,128)} %bitcast.3, bf16[3584,256]{1,0:T(8,128)(2,1)} %wg_in.1, bf16[3584,256]{1,0:T(8,128)(2,1)} %wu_in.1, bf16[256,3584]{1,0:T(8,128)(2,1)} %wd_in.1), custom_call_target="tpu_custom_call" | custom-call | tf_op jit(solution)/shard_map/pallas_call | solution.py:534
  124.2 2.2 %copy.9 = bf16[128,3584]{1,0:T(8,128)(2,1)} copy(bf16[128,3584]{1,0:T(8,128)(2,1)} %shard_map.73) | data formatting | bytes 1835008

commit v4 on v3

--- a/solution.py
+++ b/solution.py
@@ -297,6 +297,8 @@
     events.append((ready, 3, all_slices))
     for step in range(experts):
         there = max(step / last, 0.12)
+        if step == last and last >= 2:
+            continue
         if there >= ready:
             events.append((there, 4, functools.partial(hidden_step, step, mem, mem_c, span)))
         else:
@@ -335,7 +337,7 @@
     tile = 256
 
     def out_copy(block, index, upward, landing, packed):
-        part = pl.ds(index * cols, cols)
+        part = pl.ds(pl.multiple_of(index * cols, cols), cols)
         height = pl.ds(0, capacity if packed else rows)
         into = block
         if not upward:
@@ -389,7 +391,8 @@
 
         @pl.when(first)
         def _():
-            if index == 0:
+            @pl.when(index == 0)
+            def _():
                 picks = packing(block, exp)
                 for slot in range(span):
                     act[slot, block, pl.ds(0, capacity)] = jnp.dot(
@@ -427,19 +430,37 @@
         def _():
             out_copy(block, index, upward, False, False).start()
 
+    ahead = 4
+    upper = 2 * exp >= experts
+
+    def swapped(block, reach):
+        return jnp.where(jnp.logical_and(reach >= 2, jnp.logical_and(block >= 0, block <= 1)), 1 - block, block)
+
     def return_step(step, carry):
-        low = exp - (experts - step)
-        high = exp + (experts - step)
-        for index in range(OUT_PIECES):
-
-            @pl.when(low >= 0)
+        if last >= 2:
+
+            @pl.when(step == 2)
             def _():
-                send_result(jnp.maximum(low, 0), index, False)
-
-            @pl.when(high <= last)
+                hidden_step(last, mem, mem_c, span)
+
+        low = swapped(exp - (experts - step), exp)
+        high = last - swapped(last - exp - (experts - step), last - exp)
+
+        def turn(t, inner):
+            low_at = jnp.where(upper, t, t - ahead)
+            high_at = jnp.where(upper, t - ahead, t)
+
+            @pl.when(jnp.logical_and(low >= 0, jnp.logical_and(low_at >= 0, low_at < OUT_PIECES)))
             def _():
-                send_result(jnp.minimum(high, last), index, True)
-
+                send_result(jnp.maximum(low, 0), jnp.clip(low_at, 0, OUT_PIECES - 1), False)
+
+            @pl.when(jnp.logical_and(high <= last, jnp.logical_and(high_at >= 0, high_at < OUT_PIECES)))
+            def _():
+                send_result(jnp.minimum(high, last), jnp.clip(high_at, 0, OUT_PIECES - 1), True)
+
+            return inner
+
+        lax.fori_loop(0, OUT_PIECES + ahead, turn, 0)
         return carry
 
     lax.fori_loop(1, experts, return_step, 0)

time: 127 us -> 134 us (1.055); the launches traced: 126 us -> 132 us
  Pallas kernels: 124 us -> 129 us
    pallas_call x1, Pallas kernels: 124 us -> 129 us  [shards(): pl.pallas_call(functools.partial(kernel, groups, experts, span, capacity)...]
where the time goes in v4:
time: 134 us; the launch traced here: 132 us
  Pallas kernels  129 us (96%)
  local copies, waits for them, and re-layouts  2.16 us (2%)
    pallas_call x1, Pallas kernels, shards(): pl.pallas_call(functools.partial(kernel, groups, experts, span, capacity)...  129 us

profile of v4, /device:TPU:17, one launch (start us, length us, event | category | flops | bytes accessed | tf_op | source)
XLA Modules:
  0.0 131.6 jit_solution(17178273403429329296)
XLA Ops:
  0.0 129.4 %shard_map.73 = bf16[128,3584]{1,0:T(8,128)(2,1)} custom-call(bf16[128,3584]{1,0:T(8,128)(2,1)} %res_ref.1, f32[3584]{0:T(1024)} %gain_ref.1, bf16[4,3584]{1,0:T(4,128)(2,1)} %bitcast.2, s32[2,128]{1,0:T(2,128)} %bitcast.3, bf16[3584,256]{1,0:T(8,128)(2,1)} %wg_in.1, bf16[3584,256]{1,0:T(8,128)(2,1)} %wu_in.1, bf16[256,3584]{1,0:T(8,128)(2,1)} %wd_in.1), custom_call_target="tpu_custom_call" | custom-call | tf_op jit(solution)/shard_map/pallas_call | solution.py:555
  129.4 2.2 %copy.9 = bf16[128,3584]{1,0:T(8,128)(2,1)} copy(bf16[128,3584]{1,0:T(8,128)(2,1)} %shard_map.73) | data formatting | bytes 1835008
